TPU v7x, 32 devices: a whole 2x2x4 slice. The times are simulated.
32 devices in a mesh: depth: 4 (over z), tile: 8 (over y, x, core).
Axes of the slice: x: 2, y: 2, z: 4, core: 2. Of those that a mesh axis runs over, the one named last changes fastest.
Arguments:
- amplitude: float32 [8, 8, 256, 256], P('depth', 'tile'), may hold values from 0.7 to 1.3
- phase_map: float32 [8, 8, 256, 256], P('depth', 'tile'), may hold values from -3.140625 to 3.140625
- probe_wave: float32 [2, 128, 128], replicated, may hold values from -4 to 4
- propagator_phase: float32 [2, 128], replicated, may hold values from -3.140625 to 3.140625
- positions: int32 [8, 4, 2], P('tile'), may hold values from -64 to 192
- measured: float32 [8, 4, 128, 128], P('tile'), may hold values from 0 to 1
Outputs:
- object_gradient: float32 [2, 8, 8, 256, 256], P(None, 'depth', 'tile')
Inputs may be any that keep to these rules, and one draw needn't show every extreme that they name: `positions`: every window of 128 x 128 pixels starting at a position lies within 64 pixels of its tile.
All inputs are finite; a program needn't handle non-finite values.
Results may differ from a plain program's by a relative error of at most 0.02.
Values may be sent and summed in bfloat16 or wider, within the bound.
A program may use at most 128 MiB of HBM per device.

v0:
```python
import functools
import math

import jax
import jax.numpy as jnp
import numpy as np
from jax import lax
from jax.experimental import pallas as pl
from jax.experimental.pallas import tpu as pltpu
from jax.sharding import PartitionSpec as P

RIM = 64
LANES = 128
MESH = pl.DeviceIdType.MESH
F32 = jnp.float32
BF16 = jnp.bfloat16
DIRECTIONS = tuple((dr, dc) for dr in (-1, 0, 1) for dc in (-1, 0, 1) if (dr, dc) != (0, 0))


def dft_constants(points):
    line = np.arange(points)
    angles = (line[:, None] * line[None, :] % points) * (-2.0 * math.pi / points)
    real = np.cos(angles) / math.sqrt(points)
    imag = np.sin(angles) / math.sqrt(points)
    left = np.block([[real, -imag], [imag, real]])
    right = np.block([[real, imag], [-imag, real]])
    both = np.stack([left, right]).astype(np.float32)
    high = both.astype(BF16)
    low = (both - high.astype(np.float32)).astype(BF16)
    return np.stack([high, low], axis=1)


def cos_sin(angle):
    half = angle * 0.5
    square = half * half
    sine = F32((1.0 / 6227020800.0))
    for term in (-1 / 39916800.0, 1 / 362880.0, -1 / 5040.0, 1 / 120.0, -1 / 6.0, 1.0):
        sine = sine * square + F32(term)
    sine = sine * half
    cosine = F32(1 / 479001600.0)
    for term in (-1 / 3628800.0, 1 / 40320.0, -1 / 720.0, 1 / 24.0, -0.5, 1.0):
        cosine = cosine * square + F32(term)
    return 1.0 - 2.0 * sine * sine, 2.0 * sine * cosine


def dot(a, b):
    return jnp.dot(a, b, preferred_element_type=F32)


def split(value):
    high = value.astype(BF16)
    return high, (value - high.astype(F32)).astype(BF16)


def right_product(real, imag, high, low):
    points = real.shape[-1]
    x_high, x_low = split(jnp.concatenate([real, imag], axis=1))
    result = dot(x_high, high) + (dot(x_low, high) + dot(x_high, low))
    return result[:, :points], result[:, points:]


def left_product(high, low, real, imag):
    points = real.shape[0]
    v_high, v_low = split(jnp.concatenate([real, imag], axis=0))
    both = dot(high, jnp.concatenate([v_high, v_low], axis=1))
    result = both[:, :points] + (both[:, points:] + dot(low, v_high))
    return result[:points], result[points:]


def kernel(
    depth_count,
    tile_count,
    columns,
    pos_ref,
    amp_ref,
    phase_ref,
    probe_ref,
    prop_ref,
    meas_ref,
    dft_ref,
    out_ref,
    ext,
    cut_row,
    cut_col,
    put_row,
    put_col,
    mats,
    psend,
    pat,
    kept,
    back,
    csend,
    cin,
    grad,
    *rest,
):
    rim_send, rim_recv = rest[:8], rest[8:16]
    halo_s, halo_r, pat_s, pat_r, con_s, con_r, fold_s, fold_r = rest[16:]
    group, size = amp_ref.shape[0], amp_ref.shape[-1]
    waves, points = meas_ref.shape[0], meas_ref.shape[-1]
    slices = group * depth_count
    height = size + 2 * RIM
    width = size + 2 * LANES
    rows = tile_count // columns
    d = lax.axis_index("depth")
    t = lax.axis_index("tile")
    row, col = t // columns, t % columns

    def exists(dr, dc):
        return (row + dr >= 0) & (row + dr < rows) & (col + dc >= 0) & (col + dc < columns)

    def neighbour(dr, dc):
        return {"depth": d, "tile": t + dr * columns + dc}

    barrier = pltpu.get_barrier_semaphore()
    mates = [lax.rem(d + k, depth_count) for k in range(1, depth_count)]
    for mate in mates:
        pl.semaphore_signal(barrier, inc=1, device_id={"depth": mate, "tile": t}, device_id_type=MESH)
    for dr, dc in DIRECTIONS:

        @pl.when(exists(dr, dc))
        def _():
            pl.semaphore_signal(barrier, inc=1, device_id=neighbour(dr, dc), device_id_type=MESH)

    rows_in = {-1: (0, RIM), 0: (RIM, size), 1: (RIM + size, RIM)}
    cols_in = {-1: (0, LANES), 0: (LANES, size), 1: (LANES + size, LANES)}
    rows_own = {-1: (RIM, RIM), 0: (RIM, size), 1: (size, RIM)}
    cols_own = {-1: (LANES, LANES), 0: (LANES, size), 1: (size, LANES)}

    def halo_copy(i, k):
        dr, dc = DIRECTIONS[k]
        back_k = DIRECTIONS.index((-dr, -dc))
        return pltpu.make_async_remote_copy(
            src_ref=ext.at[i, :, pl.ds(*rows_own[dr]), pl.ds(*cols_own[dc])],
            dst_ref=ext.at[i, :, pl.ds(*rows_in[-dr]), pl.ds(*cols_in[-dc])],
            send_sem=halo_s.at[i, k],
            recv_sem=halo_r.at[i, back_k],
            device_id=neighbour(dr, dc),
            device_id_type=MESH,
        )

    def halo_arrival(i, k):
        dr, dc = DIRECTIONS[k]
        region = ext.at[i, :, pl.ds(*rows_in[dr]), pl.ds(*cols_in[dc])]
        return pltpu.make_async_remote_copy(
            src_ref=region,
            dst_ref=region,
            send_sem=halo_s.at[i, k],
            recv_sem=halo_r.at[i, k],
            device_id=neighbour(dr, dc),
            device_id_type=MESH,
        )

    for i in range(group):
        cosine, sine = cos_sin(phase_ref[i, 0])
        ext[i, 0, RIM : RIM + size, LANES : LANES + size] = (amp_ref[i, 0] * cosine).astype(BF16)
        ext[i, 1, RIM : RIM + size, LANES : LANES + size] = (amp_ref[i, 0] * sine).astype(BF16)
        if i == 0:
            peers = depth_count - 1
            for dr, dc in DIRECTIONS:
                peers += exists(dr, dc).astype(jnp.int32)
            pl.semaphore_wait(barrier, peers)

        for k, (dr, dc) in enumerate(DIRECTIONS):

            @pl.when(exists(dr, dc))
            def _():
                halo_copy(i, k).start()

            @pl.when(jnp.logical_not(exists(dr, dc)))
            def _():
                r0, rn = rows_in[dr]
                c0, cn = cols_in[dc]
                ext[i, :, r0 : r0 + rn, c0 : c0 + cn] = jnp.zeros((2, rn, cn), BF16)

    def one_hot(shape, shifted_axis, shift):
        along = lax.broadcasted_iota(jnp.int32, shape, shifted_axis)
        other = lax.broadcasted_iota(jnp.int32, shape, 1 - shifted_axis)
        return jnp.where(along == other + shift, F32(1), F32(0)).astype(BF16)

    for w in range(waves):
        r = pos_ref[0, 0, w] + RIM
        c = pos_ref[0, 1, w] + LANES
        span = slice(w * points, (w + 1) * points)
        cut_row[span, :] = one_hot((points, height), 1, r)
        cut_col[w] = one_hot((width, points), 0, c)
        put_row[:, span] = one_hot((height, points), 0, r)
        put_col[w] = one_hot((points, width), 1, c)

    f_left_h, f_left_l = dft_ref[0, 0], dft_ref[0, 1]
    f_right_h, f_right_l = dft_ref[1, 0], dft_ref[1, 1]
    f_full = f_right_h.astype(F32) + f_right_l.astype(F32)
    f_real, f_imag = f_full[:points, :points], f_full[:points, points:]

    def propagator(axis, sign):
        cosine, sine = cos_sin(prop_ref[axis : axis + 1, :])
        sine = sine * sign
        a_real = f_real * cosine + f_imag * sine
        a_imag = f_real * sine - f_imag * cosine
        return right_product(a_real, a_imag, f_right_h, f_right_l)

    def keep(n, top_right, bottom_left, real):
        high, low = split(
            jnp.concatenate(
                [
                    jnp.concatenate([real, top_right], axis=1),
                    jnp.concatenate([bottom_left, real], axis=1),
                ],
                axis=0,
            )
        )
        mats[n, 0] = high
        mats[n, 1] = low

    real, imag = propagator(0, 1.0)
    keep(0, -imag, imag, real)
    real, imag = propagator(1, -1.0)
    keep(1, -imag, imag, real)
    real, imag = propagator(0, -1.0)
    keep(2, -imag, imag, real)
    real, imag = propagator(1, 1.0)
    keep(3, -imag, imag, real)

    def patch_copy(i, k):
        mate = mates[k]
        return pltpu.make_async_remote_copy(
            src_ref=psend.at[mate, i],
            dst_ref=pat.at[d * group + i],
            send_sem=pat_s.at[i, k],
            recv_sem=pat_r.at[d * group + i],
            device_id={"depth": mate, "tile": t},
            device_id_type=MESH,
        )

    for i in range(group):
        for k, (dr, dc) in enumerate(DIRECTIONS):

            @pl.when(exists(dr, dc))
            def _():
                halo_arrival(i, k).wait_recv()

        bands = [dot(cut_row[...], ext[i, c]).astype(BF16) for c in range(2)]
        for w in range(waves):
            span = slice(w * points, (w + 1) * points)
            both = jnp.concatenate([bands[0][span], bands[1][span]], axis=0)
            cut = dot(both, cut_col[w]).astype(BF16)
            psend[w, i, 0] = cut[:points]
            psend[w, i, 1] = cut[points:]
        for k in range(depth_count - 1):
            patch_copy(i, k).start()
        pat[d * group + i] = psend[d, i]

    def await_patch(s):
        @pl.when(s // group != d)
        def _():
            pltpu.make_async_remote_copy(
                src_ref=pat.at[s],
                dst_ref=pat.at[s],
                send_sem=pat_s.at[0, 0],
                recv_sem=pat_r.at[s],
                device_id={"depth": mates[0], "tile": t},
                device_id_type=MESH,
            ).wait_recv()

    def mixed(s):
        p_real, p_imag = pat[s, 0].astype(F32), pat[s, 1].astype(F32)
        w_real, w_imag = kept[s, 0], kept[s, 1]
        return p_real * w_real - p_imag * w_imag, p_real * w_imag + p_imag * w_real

    kept[0] = probe_ref[...]

    def forward(s, carry):
        await_patch(s)
        real, imag = mixed(s)
        real, imag = right_product(real, imag, mats[1, 0], mats[1, 1])
        real, imag = left_product(mats[0, 0], mats[0, 1], real, imag)
        kept[s + 1, 0] = real
        kept[s + 1, 1] = imag
        return carry

    lax.fori_loop(0, slices - 1, forward, 0)
    last = slices - 1
    await_patch(last)

    def contribution_copy(s):
        return pltpu.make_async_remote_copy(
            src_ref=csend.at[s],
            dst_ref=cin.at[s % group, d],
            send_sem=con_s.at[s],
            recv_sem=con_r.at[s % group, d],
            device_id={"depth": s // group, "tile": t},
            device_id_type=MESH,
        )

    def contribute(s, s_real, s_imag):
        w_real, w_imag = kept[s, 0], kept[s, 1]
        csend[s, 0] = (w_real * s_real + w_imag * s_imag).astype(BF16)
        csend[s, 1] = (w_real * s_imag - w_imag * s_real).astype(BF16)

        @pl.when(s // group != d)
        def _():
            contribution_copy(s).start()

        @pl.when(s // group == d)
        def _():
            cin[s % group, d] = csend[s]

        p_real, p_imag = pat[s, 0].astype(F32), pat[s, 1].astype(F32)
        back[0] = p_real * s_real + p_imag * s_imag
        back[1] = p_real * s_imag - p_imag * s_real

    real, imag = mixed(last)
    real, imag = right_product(real, imag, f_right_h, f_right_l)
    real, imag = left_product(f_left_h, f_left_l, real, imag)
    misfit = real * real + imag * imag - meas_ref[d]
    real, imag = right_product(misfit * real, misfit * imag, f_left_h, f_left_l)
    real, imag = left_product(f_right_h, f_right_l, real, imag)
    contribute(last, real, imag)

    def backward(number, carry):
        s = last - 1 - number
        real, imag = right_product(back[0], back[1], mats[3, 0], mats[3, 1])
        real, imag = left_product(mats[2, 0], mats[2, 1], real, imag)
        contribute(s, real, imag)
        return carry

    lax.fori_loop(0, slices - 1, backward, 0)

    def fold_copy(i, k):
        dr, dc = DIRECTIONS[k]
        back_k = DIRECTIONS.index((-dr, -dc))
        return pltpu.make_async_remote_copy(
            src_ref=rim_send[k].at[i],
            dst_ref=rim_recv[back_k].at[i],
            send_sem=fold_s.at[i, k],
            recv_sem=fold_r.at[i, back_k],
            device_id=neighbour(dr, dc),
            device_id_type=MESH,
        )

    def fold_arrival(i, k):
        dr, dc = DIRECTIONS[k]
        return pltpu.make_async_remote_copy(
            src_ref=rim_recv[k].at[i],
            dst_ref=rim_recv[k].at[i],
            send_sem=fold_s.at[i, k],
            recv_sem=fold_r.at[i, k],
            device_id=neighbour(dr, dc),
            device_id_type=MESH,
        )

    for i in reversed(range(group)):
        for w in range(waves):

            @pl.when(d != w)
            def _():
                pltpu.make_async_remote_copy(
                    src_ref=cin.at[i, w],
                    dst_ref=cin.at[i, w],
                    send_sem=con_s.at[0],
                    recv_sem=con_r.at[i, w],
                    device_id={"depth": mates[0], "tile": t},
                    device_id_type=MESH,
                ).wait_recv()

        for c in range(2):
            spread = [dot(cin[i, w, c], put_col[w]).astype(BF16) for w in range(waves)]
            grad[c] = dot(put_row[...], jnp.concatenate(spread, axis=0))
            out_ref[c, i, 0] = grad[c, RIM : RIM + size, LANES : LANES + size]
            for k, (dr, dc) in enumerate(DIRECTIONS):
                r0, rn = rows_in[dr]
                c0, cn = cols_in[dc]
                rim_send[k][i, c] = grad[c, r0 : r0 + rn, c0 : c0 + cn].astype(BF16)
        for k, (dr, dc) in enumerate(DIRECTIONS):

            @pl.when(exists(dr, dc))
            def _():
                fold_copy(i, k).start()

    add_row = {-1: 0, 0: 0, 1: size - RIM}
    add_col = {-1: 0, 0: 0, 1: size - LANES}
    for i in reversed(range(group)):
        for k, (dr, dc) in enumerate(DIRECTIONS):

            @pl.when(exists(dr, dc))
            def _():
                fold_arrival(i, k).wait_recv()
                r0, rn = add_row[dr], rows_in[dr][1]
                c0, cn = add_col[dc], cols_in[dc][1]
                for c in range(2):
                    out_ref[c, i, 0, r0 : r0 + rn, c0 : c0 + cn] += rim_recv[k][i, c].astype(F32)

    for i in range(group):
        for k in range(depth_count - 1):
            patch_copy(i, k).wait_send()
        for k, (dr, dc) in enumerate(DIRECTIONS):

            @pl.when(exists(dr, dc))
            def _():
                halo_copy(i, k).wait_send()
                fold_copy(i, k).wait_send()

    for s in range(slices):

        @pl.when(d != s // group)
        def _():
            contribution_copy(s).wait_send()


def shards(depth_count, tile_count, amplitude, phase_map, probe_wave, propagator_phase, positions, measured):
    columns = max(2, tile_count // 8)
    group, size = amplitude.shape[0], amplitude.shape[-1]
    points = probe_wave.shape[-1]
    waves = positions.shape[1]
    slices = group * depth_count
    assert waves == depth_count
    height, width = size + 2 * RIM, size + 2 * LANES
    rims = []
    for dr, dc in DIRECTIONS:
        shape = (group, 2, RIM if dr else size, LANES if dc else size)
        rims.append(pltpu.VMEM(shape, BF16))
    dma = pltpu.SemaphoreType.DMA
    vmem = pl.BlockSpec(memory_space=pltpu.VMEM)
    return pl.pallas_call(
        functools.partial(kernel, depth_count, tile_count, columns),
        out_shape=jax.ShapeDtypeStruct((2, group, 1, size, size), F32),
        in_specs=[pl.BlockSpec(memory_space=pltpu.SMEM)] + [vmem] * 6,
        out_specs=vmem,
        scratch_shapes=[
            pltpu.VMEM((group, 2, height, width), BF16),
            pltpu.VMEM((waves * points, height), BF16),
            pltpu.VMEM((waves, width, points), BF16),
            pltpu.VMEM((height, waves * points), BF16),
            pltpu.VMEM((waves, points, width), BF16),
            pltpu.VMEM((4, 2, 2 * points, 2 * points), BF16),
            pltpu.VMEM((waves, group, 2, points, points), BF16),
            pltpu.VMEM((slices, 2, points, points), BF16),
            pltpu.VMEM((slices, 2, points, points), F32),
            pltpu.VMEM((2, points, points), F32),
            pltpu.VMEM((slices, 2, points, points), BF16),
            pltpu.VMEM((group, waves, 2, points, points), BF16),
            pltpu.VMEM((2, height, width), F32),
            *rims,
            *rims,
            dma((group, 8)),
            dma((group, 8)),
            dma((group, depth_count)),
            dma((slices,)),
            dma((slices,)),
            dma((group, waves)),
            dma((group, 8)),
            dma((group, 8)),
        ],
        compiler_params=pltpu.CompilerParams(collective_id=0, has_side_effects=True),
    )(
        jnp.transpose(positions, (0, 2, 1)),
        amplitude,
        phase_map,
        probe_wave,
        propagator_phase,
        measured[0],
        jnp.asarray(dft_constants(points)),
    )


def solution(mesh):
    in_specs = (
        P("depth", "tile", None, None),
        P("depth", "tile", None, None),
        P(),
        P(),
        P("tile", None, None),
        P("tile", None, None, None),
    )
    out_specs = P(None, "depth", "tile", None, None)
    body = functools.partial(shards, mesh.shape["depth"], mesh.shape["tile"])
    return jax.shard_map(body, mesh=mesh, in_specs=in_specs, out_specs=out_specs, check_vma=False)
```

profile of v0, /device:TPU:7, one launch (start us, length us, event | category | flops | bytes accessed | tf_op | source)
XLA Modules:
  0.0 55.7 jit_solution(15473871222352696361)
XLA Ops:
  0.0 53.4 %shard_map.73 = f32[2,2,1,256,256]{4,3,2,1,0:T(8,128)} custom-call(s32[1,2,4]{2,1,0:T(2,128)} %bitcast.3, f32[2,1,256,256]{3,2,1,0:T(8,128)} %amp_ref.1, f32[2,1,256,256]{3,2,1,0:T(8,128)} %phase_ref.1, f32[2,128,128]{2,1,0:T(8,128)} %probe_ref.1, f32[2,128]{1,0:T(2,128)} %prop_ref.1, f32[4,128,128]{2,1,0:T(8,128)} %bitcast.2, ...), custom_call_target="tpu_custom_call" | custom-call | tf_op jit(solution)/shard_map/pallas_call | solution.py:424
  53.4 2.3 %copy.9 = f32[2,2,1,256,256]{4,3,2,1,0:T(8,128)} copy(f32[2,2,1,256,256]{4,3,2,1,0:T(8,128)} %shard_map.73) | data formatting | bytes 2097152
where the time goes:
time: 55.9 us; the launch traced here: 55.7 us
  Pallas kernels  53.4 us (96%)
  local copies, waits for them, and re-layouts  2.29 us (4%)
    pallas_call x1, Pallas kernels, shards(): pl.pallas_call(functools.partial(kernel, depth_count, tile_count, columns...  53.4 us
    unnamed x1, local copies, waits for them, and re-layouts  2.29 us

commit v1 on v0

--- a/solution.py
+++ b/solution.py
@@ -14,7 +14,8 @@
 MESH = pl.DeviceIdType.MESH
 F32 = jnp.float32
 BF16 = jnp.bfloat16
-DIRECTIONS = tuple((dr, dc) for dr in (-1, 0, 1) for dc in (-1, 0, 1) if (dr, dc) != (0, 0))
+SIDES = ((0, -1), (0, 1), (-1, 0), (1, 0))
+DIRECTIONS = ((-1, 0), (1, 0), (0, -1), (0, 1)) + tuple((dr, dc) for dr in (-1, 1) for dc in (-1, 1))
 
 
 def dft_constants(points):
@@ -94,8 +95,8 @@
     grad,
     *rest,
 ):
-    rim_send, rim_recv = rest[:8], rest[8:16]
-    halo_s, halo_r, pat_s, pat_r, con_s, con_r, fold_s, fold_r = rest[16:]
+    rim_send, rim_recv = rest[:4], rest[4:8]
+    halo_s, halo_r, pat_s, pat_r, con_s, con_r, fold_s, fold_r = rest[8:]
     group, size = amp_ref.shape[0], amp_ref.shape[-1]
     waves, points = meas_ref.shape[0], meas_ref.shape[-1]
     slices = group * depth_count
@@ -129,13 +130,15 @@
 
     def halo_copy(i, k):
         dr, dc = DIRECTIONS[k]
-        back_k = DIRECTIONS.index((-dr, -dc))
+        corner = dr != 0 and dc != 0
+        far_row = dr if corner else -dr
+        back_k = DIRECTIONS.index((far_row, -dc))
         return pltpu.make_async_remote_copy(
-            src_ref=ext.at[i, :, pl.ds(*rows_own[dr]), pl.ds(*cols_own[dc])],
-            dst_ref=ext.at[i, :, pl.ds(*rows_in[-dr]), pl.ds(*cols_in[-dc])],
+            src_ref=ext.at[i, :, pl.ds(*(rows_in if corner else rows_own)[dr]), pl.ds(*cols_own[dc])],
+            dst_ref=ext.at[i, :, pl.ds(*rows_in[far_row]), pl.ds(*cols_in[-dc])],
             send_sem=halo_s.at[i, k],
             recv_sem=halo_r.at[i, back_k],
-            device_id=neighbour(dr, dc),
+            device_id=neighbour(0 if corner else dr, dc),
             device_id_type=MESH,
         )
 
@@ -163,9 +166,11 @@
 
         for k, (dr, dc) in enumerate(DIRECTIONS):
 
-            @pl.when(exists(dr, dc))
-            def _():
-                halo_copy(i, k).start()
+            if dr == 0 or dc == 0:
+
+                @pl.when(exists(dr, dc))
+                def _():
+                    halo_copy(i, k).start()
 
             @pl.when(jnp.logical_not(exists(dr, dc)))
             def _():
@@ -233,11 +238,23 @@
         )
 
     for i in range(group):
+        for dr in (-1, 1):
+
+            @pl.when(exists(dr, 0))
+            def _():
+                halo_arrival(i, DIRECTIONS.index((dr, 0))).wait_recv()
+                for dc in (-1, 1):
+
+                    @pl.when(exists(0, dc))
+                    def _():
+                        halo_copy(i, DIRECTIONS.index((dr, dc))).start()
+
         for k, (dr, dc) in enumerate(DIRECTIONS):
-
-            @pl.when(exists(dr, dc))
-            def _():
-                halo_arrival(i, k).wait_recv()
+            if dc != 0:
+
+                @pl.when(exists(dr, dc))
+                def _():
+                    halo_arrival(i, k).wait_recv()
 
         bands = [dot(cut_row[...], ext[i, c]).astype(BF16) for c in range(2)]
         for w in range(waves):
@@ -327,8 +344,8 @@
     lax.fori_loop(0, slices - 1, backward, 0)
 
     def fold_copy(i, k):
-        dr, dc = DIRECTIONS[k]
-        back_k = DIRECTIONS.index((-dr, -dc))
+        dr, dc = SIDES[k]
+        back_k = SIDES.index((-dr, -dc))
         return pltpu.make_async_remote_copy(
             src_ref=rim_send[k].at[i],
             dst_ref=rim_recv[back_k].at[i],
@@ -339,7 +356,7 @@
         )
 
     def fold_arrival(i, k):
-        dr, dc = DIRECTIONS[k]
+        dr, dc = SIDES[k]
         return pltpu.make_async_remote_copy(
             src_ref=rim_recv[k].at[i],
             dst_ref=rim_recv[k].at[i],
@@ -366,29 +383,47 @@
         for c in range(2):
             spread = [dot(cin[i, w, c], put_col[w]).astype(BF16) for w in range(waves)]
             grad[c] = dot(put_row[...], jnp.concatenate(spread, axis=0))
-            out_ref[c, i, 0] = grad[c, RIM : RIM + size, LANES : LANES + size]
-            for k, (dr, dc) in enumerate(DIRECTIONS):
-                r0, rn = rows_in[dr]
+            for k, (dr, dc) in enumerate(SIDES[:2]):
                 c0, cn = cols_in[dc]
-                rim_send[k][i, c] = grad[c, r0 : r0 + rn, c0 : c0 + cn].astype(BF16)
-        for k, (dr, dc) in enumerate(DIRECTIONS):
+                rim_send[k][i, c] = grad[c, :, c0 : c0 + cn].astype(BF16)
+        for k, (dr, dc) in enumerate(SIDES[:2]):
 
             @pl.when(exists(dr, dc))
             def _():
                 fold_copy(i, k).start()
 
-    add_row = {-1: 0, 0: 0, 1: size - RIM}
-    add_col = {-1: 0, 0: 0, 1: size - LANES}
-    for i in reversed(range(group)):
-        for k, (dr, dc) in enumerate(DIRECTIONS):
+        for k, (dr, dc) in enumerate(SIDES[:2]):
 
             @pl.when(exists(dr, dc))
             def _():
                 fold_arrival(i, k).wait_recv()
-                r0, rn = add_row[dr], rows_in[dr][1]
-                c0, cn = add_col[dc], cols_in[dc][1]
+                c0, cn = cols_own[dc]
                 for c in range(2):
-                    out_ref[c, i, 0, r0 : r0 + rn, c0 : c0 + cn] += rim_recv[k][i, c].astype(F32)
+                    grad[c, :, c0 : c0 + cn] += rim_recv[k][i, c].astype(F32)
+
+        for k, (dr, dc) in enumerate(SIDES):
+            if dr:
+                r0, rn = rows_in[dr]
+                for c in range(2):
+                    rim_send[k][i, c] = grad[c, r0 : r0 + rn, LANES : LANES + size].astype(BF16)
+
+                @pl.when(exists(dr, dc))
+                def _():
+                    fold_copy(i, k).start()
+
+        for c in range(2):
+            out_ref[c, i, 0] = grad[c, RIM : RIM + size, LANES : LANES + size]
+
+    for i in reversed(range(group)):
+        for k, (dr, dc) in enumerate(SIDES):
+            if dr:
+
+                @pl.when(exists(dr, dc))
+                def _():
+                    fold_arrival(i, k).wait_recv()
+                    r0 = 0 if dr < 0 else size - RIM
+                    for c in range(2):
+                        out_ref[c, i, 0, r0 : r0 + RIM, :] += rim_recv[k][i, c].astype(F32)
 
     for i in range(group):
         for k in range(depth_count - 1):
@@ -398,7 +433,8 @@
             @pl.when(exists(dr, dc))
             def _():
                 halo_copy(i, k).wait_send()
-                fold_copy(i, k).wait_send()
+                if k < len(SIDES):
+                    fold_copy(i, SIDES.index((dr, dc))).wait_send()
 
     for s in range(slices):
 
@@ -416,8 +452,8 @@
     assert waves == depth_count
     height, width = size + 2 * RIM, size + 2 * LANES
     rims = []
-    for dr, dc in DIRECTIONS:
-        shape = (group, 2, RIM if dr else size, LANES if dc else size)
+    for dr, dc in SIDES:
+        shape = (group, 2, RIM if dr else height, size if dr else LANES)
         rims.append(pltpu.VMEM(shape, BF16))
     dma = pltpu.SemaphoreType.DMA
     vmem = pl.BlockSpec(memory_space=pltpu.VMEM)
@@ -448,8 +484,8 @@
             dma((slices,)),
             dma((slices,)),
             dma((group, waves)),
-            dma((group, 8)),
-            dma((group, 8)),
+            dma((group, 4)),
+            dma((group, 4)),
         ],
         compiler_params=pltpu.CompilerParams(collective_id=0, has_side_effects=True),
     )(

time: 55.9 us -> 55.2 us (0.987)
  Pallas kernels: 53.4 us -> 52.7 us
    pallas_call x1, Pallas kernels: 53.4 us -> 52.7 us  [shards(): pl.pallas_call(functools.partial(kernel, depth_count, tile_count, columns...]
where the time goes in v1:
time: 55.2 us; the launch traced here: 55 us
  Pallas kernels  52.7 us (95%)
  local copies, waits for them, and re-layouts  2.29 us (4%)
    pallas_call x1, Pallas kernels, shards(): pl.pallas_call(functools.partial(kernel, depth_count, tile_count, columns...  52.7 us
    unnamed x1, local copies, waits for them, and re-layouts  2.29 us

profile of v1, /device:TPU:7, one launch (start us, length us, event | category | flops | bytes accessed | tf_op | source)
XLA Modules:
  0.0 55.0 jit_solution(13849142329853586495)
XLA Ops:
  0.0 52.7 %shard_map.73 = f32[2,2,1,256,256]{4,3,2,1,0:T(8,128)} custom-call(s32[1,2,4]{2,1,0:T(2,128)} %bitcast.3, f32[2,1,256,256]{3,2,1,0:T(8,128)} %amp_ref.1, f32[2,1,256,256]{3,2,1,0:T(8,128)} %phase_ref.1, f32[2,128,128]{2,1,0:T(8,128)} %probe_ref.1, f32[2,128]{1,0:T(2,128)} %prop_ref.1, f32[4,128,128]{2,1,0:T(8,128)} %bitcast.2, ...), custom_call_target="tpu_custom_call" | custom-call | tf_op jit(solution)/shard_map/pallas_call | solution.py:460
  52.7 2.3 %copy.9 = f32[2,2,1,256,256]{4,3,2,1,0:T(8,128)} copy(f32[2,2,1,256,256]{4,3,2,1,0:T(8,128)} %shard_map.73) | data formatting | bytes 2097152

commit v2 on v1

--- a/solution.py
+++ b/solution.py
@@ -93,6 +93,7 @@
     csend,
     cin,
     grad,
+    spread,
     *rest,
 ):
     rim_send, rim_recv = rest[:4], rest[4:8]
@@ -226,14 +227,13 @@
     real, imag = propagator(1, 1.0)
     keep(3, -imag, imag, real)
 
-    def patch_copy(i, k):
-        mate = mates[k]
+    def patch_copy(i, w):
         return pltpu.make_async_remote_copy(
-            src_ref=psend.at[mate, i],
+            src_ref=psend.at[w, i],
             dst_ref=pat.at[d * group + i],
-            send_sem=pat_s.at[i, k],
+            send_sem=pat_s.at[i, w],
             recv_sem=pat_r.at[d * group + i],
-            device_id={"depth": mate, "tile": t},
+            device_id={"depth": w, "tile": t},
             device_id_type=MESH,
         )
 
@@ -256,15 +256,17 @@
                 def _():
                     halo_arrival(i, k).wait_recv()
 
-        bands = [dot(cut_row[...], ext[i, c]).astype(BF16) for c in range(2)]
-        for w in range(waves):
+        for w in reversed(range(waves)):
             span = slice(w * points, (w + 1) * points)
-            both = jnp.concatenate([bands[0][span], bands[1][span]], axis=0)
-            cut = dot(both, cut_col[w]).astype(BF16)
+            bands = [dot(cut_row[span], ext[i, c]).astype(BF16) for c in range(2)]
+            cut = dot(jnp.concatenate(bands, axis=0), cut_col[w]).astype(BF16)
             psend[w, i, 0] = cut[:points]
             psend[w, i, 1] = cut[points:]
-        for k in range(depth_count - 1):
-            patch_copy(i, k).start()
+
+            @pl.when(d != w)
+            def _():
+                patch_copy(i, w).start()
+
         pat[d * group + i] = psend[d, i]
 
     def await_patch(s):
@@ -380,17 +382,22 @@
                     device_id_type=MESH,
                 ).wait_recv()
 
+            for c in range(2):
+                span = slice(w * points, (w + 1) * points)
+                spread[c, span, :] = dot(cin[i, w, c], put_col[w]).astype(BF16)
+
+        for k, (dr, dc) in enumerate(SIDES[:2]):
+            c0, cn = cols_in[dc]
+            for c in range(2):
+                rim_send[k][i, c] = dot(put_row[...], spread[c, :, c0 : c0 + cn]).astype(BF16)
+        for k, (dr, dc) in enumerate(SIDES[:2]):
+
+            @pl.when(exists(dr, dc))
+            def _():
+                fold_copy(i, k).start()
+
         for c in range(2):
-            spread = [dot(cin[i, w, c], put_col[w]).astype(BF16) for w in range(waves)]
-            grad[c] = dot(put_row[...], jnp.concatenate(spread, axis=0))
-            for k, (dr, dc) in enumerate(SIDES[:2]):
-                c0, cn = cols_in[dc]
-                rim_send[k][i, c] = grad[c, :, c0 : c0 + cn].astype(BF16)
-        for k, (dr, dc) in enumerate(SIDES[:2]):
-
-            @pl.when(exists(dr, dc))
-            def _():
-                fold_copy(i, k).start()
+            grad[c] = dot(put_row[...], spread[c, :, LANES : LANES + size])
 
         for k, (dr, dc) in enumerate(SIDES[:2]):
 
@@ -399,20 +406,20 @@
                 fold_arrival(i, k).wait_recv()
                 c0, cn = cols_own[dc]
                 for c in range(2):
-                    grad[c, :, c0 : c0 + cn] += rim_recv[k][i, c].astype(F32)
+                    grad[c, :, c0 - LANES : c0 - LANES + cn] += rim_recv[k][i, c].astype(F32)
 
         for k, (dr, dc) in enumerate(SIDES):
             if dr:
                 r0, rn = rows_in[dr]
                 for c in range(2):
-                    rim_send[k][i, c] = grad[c, r0 : r0 + rn, LANES : LANES + size].astype(BF16)
+                    rim_send[k][i, c] = grad[c, r0 : r0 + rn].astype(BF16)
 
                 @pl.when(exists(dr, dc))
                 def _():
                     fold_copy(i, k).start()
 
         for c in range(2):
-            out_ref[c, i, 0] = grad[c, RIM : RIM + size, LANES : LANES + size]
+            out_ref[c, i, 0] = grad[c, RIM : RIM + size]
 
     for i in reversed(range(group)):
         for k, (dr, dc) in enumerate(SIDES):
@@ -426,8 +433,12 @@
                         out_ref[c, i, 0, r0 : r0 + RIM, :] += rim_recv[k][i, c].astype(F32)
 
     for i in range(group):
-        for k in range(depth_count - 1):
-            patch_copy(i, k).wait_send()
+        for w in range(waves):
+
+            @pl.when(d != w)
+            def _():
+                patch_copy(i, w).wait_send()
+
         for k, (dr, dc) in enumerate(DIRECTIONS):
 
             @pl.when(exists(dr, dc))
@@ -475,12 +486,13 @@
             pltpu.VMEM((2, points, points), F32),
             pltpu.VMEM((slices, 2, points, points), BF16),
             pltpu.VMEM((group, waves, 2, points, points), BF16),
-            pltpu.VMEM((2, height, width), F32),
+            pltpu.VMEM((2, height, size), F32),
+            pltpu.VMEM((2, waves * points, width), BF16),
             *rims,
             *rims,
             dma((group, 8)),
             dma((group, 8)),
-            dma((group, depth_count)),
+            dma((group, waves)),
             dma((slices,)),
             dma((slices,)),
             dma((group, waves)),

time: 55.2 us -> 55.6 us (level)
  no operation moved by 1% of the time
where the time goes in v2:
time: 55.6 us; the launch traced here: 55 us
  Pallas kernels  52.7 us (95%)
  local copies, waits for them, and re-layouts  2.29 us (4%)
    pallas_call x1, Pallas kernels, shards(): pl.pallas_call(functools.partial(kernel, depth_count, tile_count, columns...  52.7 us
    unnamed x1, local copies, waits for them, and re-layouts  2.29 us

profile of v2, /device:TPU:7, one launch (start us, length us, event | category | flops | bytes accessed | tf_op | source)
XLA Modules:
  0.0 55.0 jit_solution(9541296468568974269)
XLA Ops:
  0.0 52.7 %shard_map.73 = f32[2,2,1,256,256]{4,3,2,1,0:T(8,128)} custom-call(s32[1,2,4]{2,1,0:T(2,128)} %bitcast.3, f32[2,1,256,256]{3,2,1,0:T(8,128)} %amp_ref.1, f32[2,1,256,256]{3,2,1,0:T(8,128)} %phase_ref.1, f32[2,128,128]{2,1,0:T(8,128)} %probe_ref.1, f32[2,128]{1,0:T(2,128)} %prop_ref.1, f32[4,128,128]{2,1,0:T(8,128)} %bitcast.2, ...), custom_call_target="tpu_custom_call" | custom-call | tf_op jit(solution)/shard_map/pallas_call | solution.py:471
  52.7 2.3 %copy.9 = f32[2,2,1,256,256]{4,3,2,1,0:T(8,128)} copy(f32[2,2,1,256,256]{4,3,2,1,0:T(8,128)} %shard_map.73) | data formatting | bytes 2097152

commit v3 on v1

--- a/solution.py
+++ b/solution.py
@@ -412,7 +412,7 @@
                     fold_copy(i, k).start()
 
         for c in range(2):
-            out_ref[c, i, 0] = grad[c, RIM : RIM + size, LANES : LANES + size]
+            out_ref[c, i, 0] = grad[c, RIM : RIM + size, LANES : LANES + size].astype(BF16)
 
     for i in reversed(range(group)):
         for k, (dr, dc) in enumerate(SIDES):
@@ -423,7 +423,8 @@
                     fold_arrival(i, k).wait_recv()
                     r0 = 0 if dr < 0 else size - RIM
                     for c in range(2):
-                        out_ref[c, i, 0, r0 : r0 + RIM, :] += rim_recv[k][i, c].astype(F32)
+                        held = out_ref[c, i, 0, r0 : r0 + RIM, :].astype(F32)
+                        out_ref[c, i, 0, r0 : r0 + RIM, :] = (held + rim_recv[k][i, c].astype(F32)).astype(BF16)
 
     for i in range(group):
         for k in range(depth_count - 1):
@@ -459,7 +460,7 @@
     vmem = pl.BlockSpec(memory_space=pltpu.VMEM)
     return pl.pallas_call(
         functools.partial(kernel, depth_count, tile_count, columns),
-        out_shape=jax.ShapeDtypeStruct((2, group, 1, size, size), F32),
+        out_shape=jax.ShapeDtypeStruct((2, group, 1, size, size), BF16),
         in_specs=[pl.BlockSpec(memory_space=pltpu.SMEM)] + [vmem] * 6,
         out_specs=vmem,
         scratch_shapes=[
@@ -496,7 +497,7 @@
         propagator_phase,
         measured[0],
         jnp.asarray(dft_constants(points)),
-    )
+    ).astype(F32)
 
 
 def solution(mesh):

time: 55.2 us -> 54.8 us (level)
  local copies, waits for them, and re-layouts: 2.29 us -> 0 us
  other arithmetic: 0 us -> 2.1 us
    unnamed x1 -> x0, local copies, waits for them, and re-layouts: 2.29 us -> none
    convert_element_type x0 -> x1, other arithmetic: none -> 2.1 us  [shards(): return pl.pallas_call(functools.partial(kernel, depth_count, tile_count,...]
where the time goes in v3:
time: 54.8 us; the launch traced here: 54.6 us
  Pallas kernels  52.5 us (96%)
  other arithmetic  2.1 us (4%)
    pallas_call x1, Pallas kernels, shards(): pl.pallas_call(functools.partial(kernel, depth_count, tile_count, columns...  52.5 us
    convert_element_type x1, other arithmetic, shards(): return pl.pallas_call(functools.partial(kernel, depth_count, tile_count,...  2.1 us

profile of v3, /device:TPU:7, one launch (start us, length us, event | category | flops | bytes accessed | tf_op | source)
XLA Modules:
  0.0 54.6 jit_solution(16692573482526269186)
XLA Ops:
  0.0 52.5 %shard_map.73 = bf16[2,2,1,256,256]{4,3,2,1,0:T(8,128)(2,1)} custom-call(s32[1,2,4]{2,1,0:T(2,128)} %bitcast.3, f32[2,1,256,256]{3,2,1,0:T(8,128)} %amp_ref.1, f32[2,1,256,256]{3,2,1,0:T(8,128)} %phase_ref.1, f32[2,128,128]{2,1,0:T(8,128)} %probe_ref.1, f32[2,128]{1,0:T(2,128)} %prop_ref.1, f32[4,128,128]{2,1,0:T(8,128)} %bitcast.2, ...), custom_call_target="tpu_custom_call" | custom-call | tf_op jit(solution)/shard_map/pallas_call | solution.py:461
  52.5 2.1 %convert_element_type.3 = f32[2,2,1,256,256]{4,3,2,1,0:T(8,128)} convert(bf16[2,2,1,256,256]{4,3,2,1,0:T(8,128)(2,1)} %shard_map.73) | non-fusion elementwise | flops 262144 | bytes 1572864 | tf_op jit(solution)/shard_map/convert_element_type | solution.py:500
